TPU v7x, 512 devices: a whole 4x8x8 slice. The times are simulated.
512 devices in a mesh: ctx: 32 (over z_lo, y, core), dp: 16 (over x, z_hi).
Axes of the slice: x: 4, y: 8, z: 8 (z_hi: 4, z_lo: 2; z = z_hi * 2 + z_lo), core: 2. Of those that a mesh axis runs over, the one named last changes fastest.
Arguments:
- queries: bfloat16 [16, 8192, 1024], P('dp', 'ctx'), may hold values from -6 to 6
- key_vecs: bfloat16 [16, 8192, 1024], P('dp', 'ctx'), may hold values from -6 to 6
- value_vecs: bfloat16 [16, 8192, 1024], P('dp', 'ctx'), may hold values from -6 to 6
- out_grad: bfloat16 [16, 8192, 1024], P('dp', 'ctx'), may hold values from -6 to 6
- out_weight: bfloat16 [1024, 1024], P(('ctx', 'dp')), may hold values from -0.1875 to 0.1875
Outputs:
- query_grad: bfloat16 [16, 8192, 1024], P('dp', 'ctx')
- key_grad: bfloat16 [16, 8192, 1024], P('dp', 'ctx')
- value_grad: bfloat16 [16, 8192, 1024], P('dp', 'ctx')
- weight_grad: float32 [1024, 1024], P(('ctx', 'dp'))
All inputs are finite; a program needn't handle non-finite values.
Results may differ from a plain program's by a relative error of at most 0.0057.
Values may be sent and summed in bfloat16 or wider, within the bound.
A program may use at most 128 MiB of HBM per device.

v0:
```python
import math

import jax
import jax.numpy as jnp
from jax import lax
from jax.sharding import PartitionSpec as P

HEAD = 128
BLOCK = 256


def ein(form, left, right):
    return jnp.einsum(form, left, right, preferred_element_type=jnp.float32)


def per_device(queries, key_vecs, value_vecs, out_grad, out_weight):
    qry_rows = queries[0]
    tok_count = qry_rows.shape[0]
    width = qry_rows.shape[1]
    heads_n = width // HEAD
    count = tok_count // BLOCK
    n_ctx = lax.axis_size("ctx")
    n_dp = lax.axis_size("dp")
    att_scale = 1.0 / math.sqrt(HEAD * tok_count * n_ctx)
    inv_root = 1.0 / math.sqrt(n_dp * tok_count * n_ctx)
    flat_grad = out_grad[0]

    def split(array):
        return array.reshape(count, BLOCK, heads_n, HEAD)

    qry_blk = split(qry_rows)
    key_blk = split(key_vecs[0])
    val_blk = split(value_vecs[0])
    kv_block = ein("bshe,bshf->bhef", key_blk, val_blk)
    local_kv = jnp.sum(kv_block, 0)
    grad_full = lax.dot_general(
        flat_grad,
        lax.all_gather(out_weight, ("ctx", "dp"), axis=0, tiled=True),
        (((1,), (1,)), ((), ())),
        preferred_element_type=jnp.float32,
    )
    att_grad = grad_full.astype(jnp.bfloat16)
    grd_blk = split(att_grad)
    qd_block = ein("bthf,bthe->bhfe", grd_blk, qry_blk)
    local_qd = jnp.sum(qd_block, 0)
    rows_each = heads_n * HEAD // n_ctx
    kv_parts, qd_parts = (
        lax.all_to_all(
            local_kv.reshape(n_ctx, rows_each, HEAD), "ctx", split_axis=0, concat_axis=0, tiled=True
        ),
        lax.all_to_all(
            local_qd.reshape(n_ctx, rows_each, HEAD), "ctx", split_axis=0, concat_axis=0, tiled=True
        ),
    )
    kv_earlier = jnp.cumsum(kv_parts, 0) - kv_parts
    qd_later = jnp.cumsum(qd_parts[::-1], 0)[::-1] - qd_parts
    kv_back, qd_back = (
        lax.all_to_all(kv_earlier, "ctx", split_axis=0, concat_axis=0, tiled=True),
        lax.all_to_all(qd_later, "ctx", split_axis=0, concat_axis=0, tiled=True),
    )
    kv_before = kv_back.reshape(local_kv.shape)
    qd_after = qd_back.reshape(local_qd.shape)
    state_in = (kv_before[None] + jnp.cumsum(kv_block, 0) - kv_block).astype(jnp.bfloat16)
    carried = (qd_after[None] + jnp.cumsum(qd_block[::-1], 0)[::-1] - qd_block).astype(jnp.bfloat16)
    positions = jnp.arange(BLOCK)
    causal = positions[:, None] >= positions[None, :]
    scores = jnp.where(causal, ein("bthe,bshe->bhts", qry_blk, key_blk), 0.0).astype(jnp.bfloat16)
    attended = att_scale * (
        ein("bhts,bshf->bthf", scores, val_blk) + ein("bthe,bhef->bthf", qry_blk, state_in)
    )
    attended = attended.astype(jnp.bfloat16).reshape(tok_count, width)
    weight_grad = lax.psum_scatter(
        lax.dot_general(
            attended, flat_grad, (((0,), (0,)), ((), ())), preferred_element_type=jnp.float32
        )
        * inv_root,
        ("ctx", "dp"),
        scatter_dimension=0,
        tiled=True,
    )
    dscores = jnp.where(causal, ein("bthf,bshf->bhts", grd_blk, val_blk), 0.0).astype(jnp.bfloat16)
    query_grad = att_scale * (
        ein("bhts,bshe->bthe", dscores, key_blk) + ein("bthf,bhef->bthe", grd_blk, state_in)
    )
    key_grad = att_scale * (
        ein("bhts,bthe->bshe", dscores, qry_blk) + ein("bshf,bhfe->bshe", val_blk, carried)
    )
    value_grad = att_scale * (
        ein("bhts,bthf->bshf", scores, grd_blk) + ein("bshe,bhfe->bshf", key_blk, carried)
    )
    shape_out = (1, tok_count, width)
    return (
        query_grad.astype(jnp.bfloat16).reshape(shape_out),
        key_grad.astype(jnp.bfloat16).reshape(shape_out),
        value_grad.astype(jnp.bfloat16).reshape(shape_out),
        weight_grad,
    )


def solution(mesh):
    placed = (
        P("dp", "ctx", None),
        P("dp", "ctx", None),
        P("dp", "ctx", None),
        P("dp", "ctx", None),
        P(("ctx", "dp"), None),
    )
    return jax.shard_map(
        per_device,
        mesh=mesh,
        in_specs=placed,
        out_specs=(
            P("dp", "ctx", None),
            P("dp", "ctx", None),
            P("dp", "ctx", None),
            P(("ctx", "dp"), None),
        ),
        check_vma=False,
    )
```

profile of v0, /device:TPU:1, one launch (start us, length us, event | category | flops | bytes accessed | tf_op | source)
XLA Modules:
  0.0 1405.0 jit_solution(1441930087557721622)
XLA Ops:
  7.2 0.0 copy-start
  7.2 0.0 all-gather.3.cloned.1.call-start
  7.2 0.7 all-gather.3.cloned.1.call-update
  7.9 1.2 copy.54
  9.2 1.1 copy.55
  10.3 0.3 fusion.12
  10.6 27.0 %all_to_all.20 = f32[32,32,128]{2,1,0:T(8,128)S(1)} all-to-all(f32[32,32,128]{2,1,0:T(8,128)S(1)} %bitcast.84), channel_id=1, replica_groups=mesh['ctx'=32,'dp'=16] {'ctx'}, dimensions={0} | all-to-all | bytes 1048576 | tf_op jit(solution)/shard_map/all_to_all | solution.py:48
  37.6 0.8 reduce-window_subtract_fusion
  38.5 5.7 all-to-all-start.1
  44.1 0.0 all-reduce.3.cloned.1.call-start
  44.2 1.1 copy.56
  45.3 0.0 copy-start.1
  45.4 0.5 select_convert_fusion
  45.8 0.0 copy-start.2
  45.9 1.0 copy-done.2
  46.9 1.5 convolution_bitcast_fusion.1
  48.4 12.7 all-to-all-done.1
  61.1 0.1 fusion.8
  61.1 1.6 fusion.7
  62.7 0.0 copy-done
  62.7 2.7 convolution_multiply_fusion
  65.4 0.0 all-reduce.3.cloned.1.call-update
  65.5 1003.1 %all-gather.3.cloned.1.call-done = bf16[512,2,1024]{2,1,0:T(2,128)(2,1)} async-done(((bf16[1,2,1024]{2,1,0:T(2,128)(2,1)}), bf16[512,2,1024]{2,1,0:T(2,128)(2,1)}) %all-gather.3.cloned.1.call-update) | async-done | bytes 2097168 | tf_op jit(solution)/shard_map/all_gather | solution.py:38
  1068.6 4.1 reshape.148
  1072.8 2.3 convolution_convert_fusion
  1075.1 0.2 copy.53
  1075.3 0.0 copy-done.1
  1075.3 1.1 fusion.20
  1076.4 6.8 all-to-all-start.2
  1083.3 279.0 %all-reduce.3.cloned.1.call-done = f32[1024,1024]{1,0:T(8,128)} async-done(((f32[1024,1024]{1,0:T(8,128)}), f32[1024,1024]{1,0:T(8,128)}) %all-reduce.3.cloned.1.call-update) | async-done | bytes 4194320
  1362.2 1.4 constant_dynamic-slice_fusion
  1363.6 0.5 select_convert_fusion.1
  1364.1 0.0 all-to-all-done.2
  1364.1 1.9 rev.6
  1366.0 1.1 fusion.22
  1367.1 1.9 reverse_subtract_fusion
  1369.0 7.4 all-to-all-start.3
  1376.4 0.5 convolution_bitcast_fusion.2
  1376.9 1.1 fusion.4
  1378.0 2.0 copy.48
  1380.0 0.0 copy-start.3
  1380.0 2.4 convolution_bitcast_fusion
  1382.5 0.0 copy-done.3
  1382.5 0.3 fusion.23
  1382.8 10.2 all-to-all-done.3
  1393.0 1.3 fusion.9
  1394.3 1.6 fusion.5
  1395.9 1.0 copy.49
  1396.9 0.3 fusion.6
  1397.2 1.0 copy.50
  (1 shorter events, 0.0 us)
Async XLA Ops:
  7.2 55.6 %copy-start = (bf16[1,256,1024]{2,1,0:T(8,128)(2,1)S(1)}, bf16[1,256,1024]{2,1,0:T(8,128)(2,1)}, u32[]{:S(2)}) copy-start(bf16[1,256,1024]{2,1,0:T(8,128)(2,1)} %param.8) | copy-start | bytes 1572868
  7.2 1061.4 %all-gather.3.cloned.1.call-start = ((), (), s32[]{:S(2)}) async-start(), calls=%async_computation.4 | async-start | bytes 2101248 | tf_op jit(solution)/shard_map/all_gather | solution.py:38
  38.5 22.6 %all-to-all-start.1 = ((f32[32,32,128]{2,1,0:T(8,128)}), f32[32,32,128]{2,1,0:T(8,128)S(1)}, u32[]{:S(2)}, u32[]{:S(2)}) async-start(f32[32,32,128]{2,1,0:T(8,128)} %reduce-window_subtract_fusion), calls=%async_computation.1 | async-start | bytes 1048576 | tf_op jit(solution)/shard_map/all_to_all | solution.py:58
  44.1 1318.1 %all-reduce.3.cloned.1.call-start = ((), (), s32[]{:S(2)}) async-start(), calls=%async_computation.5 | async-start | bytes 8388608
  45.3 1030.0 %copy-start.1 = (bf16[32,8,8,128]{3,2,1,0:T(8,128)(2,1)}, bf16[32,8,8,128]{3,2,1,0:T(8,128)(2,1)S(1)}, u32[]{:S(2)}) copy-start(bf16[32,8,8,128]{3,2,1,0:T(8,128)(2,1)S(1)} %copy.56) | copy-start | bytes 1572868
  45.8 1.0 copy-start.2
  1076.4 287.7 %all-to-all-start.2 = ((f32[32,32,128]{2,1,0:T(8,128)}), f32[32,32,128]{2,1,0:T(8,128)}, u32[]{:S(2)}, u32[]{:S(2)}) async-start(f32[32,32,128]{2,1,0:T(8,128)} %bitcast.9), calls=%async_computation.2 | async-start | bytes 1048576 | tf_op jit(solution)/shard_map/all_to_all | solution.py:51
  1369.0 24.1 %all-to-all-start.3 = ((f32[32,32,128]{2,1,0:T(8,128)}), f32[32,32,128]{2,1,0:T(8,128)}, u32[]{:S(2)}, u32[]{:S(2)}) async-start(f32[32,32,128]{2,1,0:T(8,128)} %reverse_subtract_fusion), calls=%async_computation.3 | async-start | bytes 1048576 | tf_op jit(solution)/shard_map/all_to_all | solution.py:59
  1380.0 2.4 copy-start.3
Sparse Core Ops, SparseCore 0:
  10.2 1058.3 all-gather.2
  1073.6 288.5 all-reduce.2
where the time goes:
time: 1410 us
  waiting for transfers between devices  1310 us (93%)
  blocking collectives  27 us (2%)
  starting transfers between devices  20 us (1%)
  matrix products  16.7 us (1%)
  local copies, waits for them, and re-layouts  16.2 us (1%)
  between operations  14.2 us (1%)
    all_gather x1, waiting for transfers between devices, per_device(): lax.all_gather(out_weight, ('ctx', 'dp'), axis=0, tiled=True)  1000 us
    unnamed x3, waiting for transfers between devices  280 us
  transfers between devices with their start and end apart: 5, of which 4 were waited for; matrix products, arithmetic and copies ran while one was open for 2% of the time, Pallas kernels for 0%

commit v1 on v0

v1 whole, which is shorter than its diff:
```python
import math

import jax
import jax.numpy as jnp
from jax import lax
from jax.experimental import pallas as pl
from jax.experimental.pallas import tpu as pltpu
from jax.sharding import PartitionSpec as P

HEAD = 128
HEADS = 8
TOK = 256
D = 1024
NX, NY, NZ = 4, 8, 8
NCTX = 32
F32, BF16 = jnp.float32, jnp.bfloat16
MESH = pl.DeviceIdType.MESH


def device(x, y, z, core):
    return (((z % 2) * NY + y) * 2 + core, x * (NZ // 2) + z // 2)


def dot(left, right, dims):
    return lax.dot_general(left, right, (dims, ((), ())), preferred_element_type=F32)


def tn(left, right):
    return dot(left, right, ((0,), (0,)))


def nt(left, right):
    return dot(left, right, ((1,), (1,)))


def nn(left, right):
    return dot(left, right, ((1,), (0,)))


def kernel(
    att_scale, inv_root,
    q_ref, k_ref, v_ref, g_ref, w_ref,
    dq_ref, dk_ref, dv_ref, wg_ref,
    tiles, weight, kv_out, kv_in, kv_sum, kv_back, qd_out, qd_in, qd_sum, qd_back,
    scores, dscores, acc, att_grad, dk_acc, dv_acc, attended,
    part, part_in, sum1, in1, sum2, in2, sum3, in3, flat,
    ag_s, ag_r, scan_s, scan_r, rs_s, rs_r,
):
    ctx, dp = lax.axis_index("ctx"), lax.axis_index("dp")
    core, y, zl = ctx % 2, (ctx // 2) % NY, ctx // (2 * NY)
    x, zh = dp // (NZ // 2), dp % (NZ // 2)
    z = zh * 2 + zl

    def at_y(o):
        return device(x, (y + o) % NY, z, core)

    def at_z(o):
        return device(x, y, (z + o) % NZ, core)

    def at_x(o):
        return device((x + o) % NX, y, z, core)

    other = device(x, y, z, 1 - core)

    def remote(src, dst, s, r, to):
        return pltpu.make_async_remote_copy(
            src_ref=src, dst_ref=dst, send_sem=s, recv_sem=r, device_id=to, device_id_type=MESH
        )

    barrier = pltpu.get_barrier_semaphore()

    def greet(o, carry):
        pl.semaphore_signal(barrier, inc=1, device_id=((ctx + o) % NCTX, dp), device_id_type=MESH)
        return carry

    lax.fori_loop(1, NCTX, greet, 0)
    for o in range(1, NX):
        pl.semaphore_signal(barrier, inc=1, device_id=at_x(o), device_id_type=MESH)
    for o in range(2, NZ):
        pl.semaphore_signal(
            barrier, inc=1, device_id=device(x, y, (z - zl + (zl + o) % 2 + (o - o % 2)) % NZ, core),
            device_id_type=MESH,
        )
    own = w_ref[...].astype(F32)
    for row in range(2):
        for cb in range(8):
            flat[row * 8 + cb : row * 8 + cb + 1, :] = own[row : row + 1, cb * 128 : cb * 128 + 128]
    tiles[zl, y, core, x, zh] = flat[...].astype(BF16)
    pl.semaphore_wait(barrier, NCTX - 1 + NX - 1 + NZ - 2)

    stage1 = [
        remote(tiles.at[zl, y, core, x, zh], tiles.at[zl, y, core, x, zh], ag_s.at[o - 1], ag_r.at[o - 1], at_y(o))
        for o in range(1, NY)
    ]
    for copy in stage1:
        copy.start()

    def exchange(src, dst, sems):
        def send(o, carry):
            to = (ctx + o) % NCTX
            remote(src.at[to], dst.at[ctx], scan_s.at[sems], scan_r.at[sems], (to, dp)).start()
            return carry

        lax.fori_loop(1, NCTX, send, 0)
        dst[ctx] = src[ctx]
        every = pl.ds(0, NCTX - 1)
        return remote(src.at[every], dst.at[every], scan_s.at[sems], scan_r.at[sems], other)

    for h in range(HEADS):
        cols = slice(h * HEAD, h * HEAD + HEAD)
        product = tn(k_ref[:, cols], v_ref[:, cols]).astype(BF16)
        kv_out[h * 4 : h * 4 + 4] = product.reshape(4, 32, HEAD)
    kv_there = exchange(kv_out, kv_in, 0)

    for copy in stage1:
        copy.wait_recv()
    column = tiles.at[zl, :, core, x, zh]
    stage2 = [
        remote(column, column, ag_s.at[6 + o], ag_r.at[6 + o], at_z(o)) for o in range(1, NZ)
    ]
    for copy in stage2:
        copy.start()

    causal = lax.broadcasted_iota(jnp.int32, (TOK, TOK), 0) >= lax.broadcasted_iota(jnp.int32, (TOK, TOK), 1)
    for h in range(HEADS):
        cols = slice(h * HEAD, h * HEAD + HEAD)
        masked = jnp.where(causal, nt(q_ref[:, cols], k_ref[:, cols]), 0.0).astype(BF16)
        scores[h] = masked
        acc[:, cols] = nn(masked, v_ref[:, cols])

    kv_there.wait_recv()
    total = jnp.zeros((32, HEAD), F32)
    for s in range(NCTX):
        kv_sum[s] = total.astype(BF16)
        total = total + kv_in[s].astype(F32)
    kv_home = exchange(kv_sum, kv_back, 1)

    for copy in stage2:
        copy.wait_recv()
    def plane(a):
        return tiles.at[:, :, core, a]

    stage3 = [
        remote(plane(x), plane(x), ag_s.at[13 + o], ag_r.at[13 + o], at_x(o)) for o in range(1, NX)
    ]
    for copy in stage3:
        copy.start()
    swaps = [
        remote(plane((x - o + NX) % NX), plane((x - o + NX) % NX), ag_s.at[17 + o], ag_r.at[17 + o], other)
        for o in range(NX)
    ]
    swaps[0].start()
    for o in range(1, NX):
        stage3[o - 1].wait_recv()
        swaps[o].start()

    rows_i = lax.broadcasted_iota(jnp.int32, (256, 256), 0)
    cols_i = lax.broadcasted_iota(jnp.int32, (256, 256), 1)

    def tile_row(i):
        return ((i & 31) >> 1) * 16 + (i & 1) * 8 + (i >> 5)

    to_rows = jnp.where(cols_i == tile_row(rows_i), 1.0, 0.0).astype(BF16)
    to_tiles = jnp.where(rows_i == tile_row(cols_i), 1.0, 0.0).astype(BF16)

    def place(which):
        def one(i, carry):
            a, b = i // NY, i % NY
            rows = nn(to_rows, tiles[a, b, which].reshape(256, 128)).astype(BF16)
            at = pl.ds(pl.multiple_of((i * 2 + which) * 32, 32), 32)
            for cb in range(8):
                weight[at, cb * 128 : cb * 128 + 128] = rows[cb * 32 : cb * 32 + 32]
            return carry

        lax.fori_loop(0, 16, one, 0)

    place(core)
    for copy in swaps:
        copy.wait_recv()
    place(1 - core)

    for h in range(HEADS):
        cols = slice(h * HEAD, h * HEAD + HEAD)
        grad = nt(g_ref[...], weight[cols, :]).astype(BF16)
        att_grad[:, cols] = grad
        product = tn(grad, q_ref[:, cols]).astype(BF16)
        qd_out[h * 4 : h * 4 + 4] = product.reshape(4, 32, HEAD)
    qd_there = exchange(qd_out, qd_in, 2)

    kv_home.wait_recv()
    pairs = []
    for h in range(HEADS):
        cols = slice(h * HEAD, h * HEAD + HEAD)
        state = kv_back[h * 4 : h * 4 + 4].reshape(HEAD, HEAD)
        mixed = (att_scale * (acc[:, cols] + nn(q_ref[:, cols], state))).astype(BF16)
        term = tn(mixed, g_ref[...]).astype(BF16)
        for b in range(4):
            rows = term[b * 32 : b * 32 + 32]
            stacked = jnp.concatenate([rows[:, cb * 128 : cb * 128 + 128] for cb in range(8)], 0)
            block = h * 4 + b
            part[block // 16, (block // 2) % 8, block % 2] = (
                nn(to_tiles, stacked).astype(BF16).reshape(NX, NZ // 2, 16, 128)
            )
        half = (h // 4, pl.ds((h % 4) * 2, 2))
        copy = remote(
            part.at[half[0], half[1], 1 - core], part_in.at[half[0], half[1]], rs_s.at[h], rs_r.at[h], other
        )
        copy.start()
        pairs.append(copy)

    for h in range(HEADS):
        cols = slice(h * HEAD, h * HEAD + HEAD)
        grad = att_grad[:, cols]
        masked = jnp.where(causal, nt(grad, v_ref[:, cols]), 0.0).astype(BF16)
        state = kv_back[h * 4 : h * 4 + 4].reshape(HEAD, HEAD)
        dq_ref[:, cols] = (att_scale * (nn(masked, k_ref[:, cols]) + nt(grad, state))).astype(BF16)
        dk_acc[:, cols] = tn(masked, q_ref[:, cols])
        dv_acc[:, cols] = tn(scores[h], grad)

    for h in range(HEADS):
        pairs[h].wait_recv()
        for b in range(2):
            a, row = h // 4, (h % 4) * 2 + b
            both = part[a, row, core].astype(F32) + part_in[a, row].astype(F32)
            sum1[:, :, a, row] = both.astype(BF16)
    by_x = []
    for o in range(1, NX):
        copy = remote(sum1.at[(x + o) % NX], in1.at[o - 1], rs_s.at[7 + o], rs_r.at[7 + o], at_x(o))
        copy.start()
        by_x.append(copy)

    qd_there.wait_recv()
    total = jnp.zeros((32, HEAD), F32)
    for s in reversed(range(NCTX)):
        qd_sum[s] = total.astype(BF16)
        total = total + qd_in[s].astype(F32)
    qd_home = exchange(qd_sum, qd_back, 3)

    for copy in by_x:
        copy.wait_recv()

    def add_x(i, carry):
        value = sum1[x, i // 2, i % 2].astype(F32)
        for o in range(NX - 1):
            value = value + in1[o, i // 2, i % 2].astype(F32)
        sum2[i] = value.astype(BF16)
        return carry

    lax.fori_loop(0, NZ, add_x, 0)
    by_z = []
    for o in range(1, NZ):
        copy = remote(sum2.at[(z + o) % NZ], in2.at[o - 1], rs_s.at[10 + o], rs_r.at[10 + o], at_z(o))
        copy.start()
        by_z.append(copy)

    qd_home.wait_recv()
    for h in range(HEADS):
        cols = slice(h * HEAD, h * HEAD + HEAD)
        carried = qd_back[h * 4 : h * 4 + 4].reshape(HEAD, HEAD)
        dk_ref[:, cols] = (att_scale * (dk_acc[:, cols] + nn(v_ref[:, cols], carried))).astype(BF16)
        dv_ref[:, cols] = (att_scale * (dv_acc[:, cols] + nt(k_ref[:, cols], carried))).astype(BF16)

    for copy in by_z:
        copy.wait_recv()
    value = sum2[z].astype(F32)
    for o in range(NZ - 1):
        value = value + in2[o].astype(F32)
    sum3[...] = value.astype(BF16)
    by_y = []
    for o in range(1, NY):
        copy = remote(sum3.at[(y + o) % NY], in3.at[o - 1], rs_s.at[17 + o], rs_r.at[17 + o], at_y(o))
        copy.start()
        by_y.append(copy)
    for copy in by_y:
        copy.wait_recv()
    value = sum3[y].astype(F32)
    for o in range(NY - 1):
        value = value + in3[o].astype(F32)
    value = value * inv_root
    for row in range(2):
        for cb in range(8):
            wg_ref[row : row + 1, cb * 128 : cb * 128 + 128] = value[row * 8 + cb : row * 8 + cb + 1, :]

    for copy in stage1 + stage2 + stage3 + swaps + pairs + by_x + by_z + by_y:
        copy.wait_send()
    for copy in (kv_there, kv_home, qd_there, qd_home):
        copy.wait_send()


def per_device(queries, key_vecs, value_vecs, out_grad, out_weight):
    att_scale = 1.0 / math.sqrt(HEAD * TOK * NCTX)
    inv_root = 1.0 / math.sqrt(16 * TOK * NCTX)

    def body(*refs):
        kernel(att_scale, inv_root, *refs)

    vmem = pl.BlockSpec(memory_space=pltpu.VMEM)
    piece = pltpu.VMEM((NCTX, 32, HEAD), BF16)
    wide = pltpu.VMEM((TOK, D), F32)
    narrow = pltpu.VMEM((TOK, D), BF16)
    out = jax.ShapeDtypeStruct((TOK, D), BF16)
    dq, dk, dv, wg = pl.pallas_call(
        body,
        out_shape=(out, out, out, jax.ShapeDtypeStruct((2, D), F32)),
        in_specs=[vmem] * 5,
        out_specs=(vmem,) * 4,
        scratch_shapes=[
            pltpu.VMEM((2, NY, 2, NX, NZ // 2, 16, 128), BF16),
            pltpu.VMEM((D, D), BF16),
            piece, piece, piece, piece, piece, piece, piece, piece,
            pltpu.VMEM((HEADS, TOK, TOK), BF16),
            pltpu.VMEM((8, 128), BF16),
            wide, narrow, wide, wide,
            pltpu.VMEM((8, 128), BF16),
            pltpu.VMEM((2, NY, 2, NX, NZ // 2, 16, 128), BF16),
            pltpu.VMEM((2, NY, NX, NZ // 2, 16, 128), BF16),
            pltpu.VMEM((NX, NZ // 2, 2, NY, 16, 128), BF16),
            pltpu.VMEM((NX - 1, NZ // 2, 2, NY, 16, 128), BF16),
            pltpu.VMEM((NZ, NY, 16, 128), BF16),
            pltpu.VMEM((NZ - 1, NY, 16, 128), BF16),
            pltpu.VMEM((NY, 16, 128), BF16),
            pltpu.VMEM((NY - 1, 16, 128), BF16),
            pltpu.VMEM((16, 128), F32),
            pltpu.SemaphoreType.DMA((21,)), pltpu.SemaphoreType.DMA((21,)),
            pltpu.SemaphoreType.DMA((4,)), pltpu.SemaphoreType.DMA((4,)),
            pltpu.SemaphoreType.DMA((25,)), pltpu.SemaphoreType.DMA((25,)),
        ],
        compiler_params=pltpu.CompilerParams(
            collective_id=0, has_side_effects=True, vmem_limit_bytes=48 << 20
        ),
        name="backward",
    )(queries[0], key_vecs[0], value_vecs[0], out_grad[0], out_weight)
    return dq[None], dk[None], dv[None], wg


def solution(mesh):
    rows = P("dp", "ctx", None)
    return jax.shard_map(
        per_device,
        mesh=mesh,
        in_specs=(rows, rows, rows, rows, P(("ctx", "dp"), None)),
        out_specs=(rows, rows, rows, P(("ctx", "dp"), None)),
        check_vma=False,
    )
```

time: 1410 us -> 94.5 us (0.07)
  the two profiles are of different devices: /device:TPU:1 before, /device:TPU:6 now
where the time goes in v1:
time: 94.5 us; the launch traced here: 94.2 us
  Pallas kernels  85.7 us (91%)
  local copies, waits for them, and re-layouts  7.82 us (8%)
    pallas_call x1, Pallas kernels, per_device(): pl.pallas_call(body, out_shape=(out, out, out, jax.ShapeDtypeStruct((2, D...  85.7 us
    unnamed x14, local copies, waits for them, and re-layouts  7.82 us

profile of v1, /device:TPU:6, one launch (start us, length us, event | category | flops | bytes accessed | tf_op | source)
XLA Modules:
  0.0 94.2 jit_solution(6257298256140563611)
XLA Ops:
  0.6 0.0 copy-start.4
  0.6 0.7 copy-done.4
  1.3 0.0 copy-start
  1.3 1.0 %copy-done = bf16[1,256,1024]{2,1,0:T(8,128)(2,1)S(1)} copy-done((bf16[1,256,1024]{2,1,0:T(8,128)(2,1)S(1)}, bf16[1,256,1024]{2,1,0:T(8,128)(2,1)}, u32[]{:S(2)}) %copy-start) | copy-done | bytes 524312
  2.4 0.0 copy-start.1
  2.4 1.0 %copy-done.1 = bf16[1,256,1024]{2,1,0:T(8,128)(2,1)S(1)} copy-done((bf16[1,256,1024]{2,1,0:T(8,128)(2,1)S(1)}, bf16[1,256,1024]{2,1,0:T(8,128)(2,1)}, u32[]{:S(2)}) %copy-start.1) | copy-done | bytes 524312
  3.4 0.0 copy-start.2
  3.4 1.0 %copy-done.2 = bf16[1,256,1024]{2,1,0:T(8,128)(2,1)S(1)} copy-done((bf16[1,256,1024]{2,1,0:T(8,128)(2,1)S(1)}, bf16[1,256,1024]{2,1,0:T(8,128)(2,1)}, u32[]{:S(2)}) %copy-start.2) | copy-done | bytes 524312
  4.4 0.0 copy-start.3
  4.4 1.0 %copy-done.3 = bf16[1,256,1024]{2,1,0:T(8,128)(2,1)S(1)} copy-done((bf16[1,256,1024]{2,1,0:T(8,128)(2,1)S(1)}, bf16[1,256,1024]{2,1,0:T(8,128)(2,1)}, u32[]{:S(2)}) %copy-start.3) | copy-done | bytes 524312
  5.5 85.7 %backward.1 = (bf16[256,1024]{1,0:T(8,128)(2,1)S(1)}, bf16[256,1024]{1,0:T(8,128)(2,1)S(1)}, bf16[256,1024]{1,0:T(8,128)(2,1)S(1)}, f32[2,1024]{1,0:T(2,128)S(1)}) custom-call(bf16[256,1024]{1,0:T(8,128)(2,1)S(1)} %bitcast.10, bf16[256,1024]{1,0:T(8,128)(2,1)S(1)} %bitcast.11, bf16[256,1024]{1,0:T(8,128)(2,1)S(1)} %bitcast.12, ...), custom_call_target="tpu_custom_call" | custom-call | tf_op jit(solution)/shard_map/backward/pallas_call | solution.py:302
  91.2 0.8 copy.13
  92.0 0.8 copy.14
  92.8 0.8 copy.15
  93.6 0.6 copy.16
Async XLA Ops:
  0.6 0.7 copy-start.4
  1.3 1.0 %copy-start = (bf16[1,256,1024]{2,1,0:T(8,128)(2,1)S(1)}, bf16[1,256,1024]{2,1,0:T(8,128)(2,1)}, u32[]{:S(2)}) copy-start(bf16[1,256,1024]{2,1,0:T(8,128)(2,1)} %param.5) | copy-start | bytes 1572868
  2.4 1.0 %copy-start.1 = (bf16[1,256,1024]{2,1,0:T(8,128)(2,1)S(1)}, bf16[1,256,1024]{2,1,0:T(8,128)(2,1)}, u32[]{:S(2)}) copy-start(bf16[1,256,1024]{2,1,0:T(8,128)(2,1)} %param.6) | copy-start | bytes 1572868
  3.4 1.0 %copy-start.2 = (bf16[1,256,1024]{2,1,0:T(8,128)(2,1)S(1)}, bf16[1,256,1024]{2,1,0:T(8,128)(2,1)}, u32[]{:S(2)}) copy-start(bf16[1,256,1024]{2,1,0:T(8,128)(2,1)} %param.7) | copy-start | bytes 1572868
  4.4 1.0 %copy-start.3 = (bf16[1,256,1024]{2,1,0:T(8,128)(2,1)S(1)}, bf16[1,256,1024]{2,1,0:T(8,128)(2,1)}, u32[]{:S(2)}) copy-start(bf16[1,256,1024]{2,1,0:T(8,128)(2,1)} %param.8) | copy-start | bytes 1572868

commit v2 on v0

v2 whole, which is shorter than its diff:
```python
import math

import jax
import jax.numpy as jnp
from jax import lax
from jax.experimental import pallas as pl
from jax.experimental.pallas import tpu as pltpu
from jax.sharding import PartitionSpec as P

HEAD = 128
HEADS = 8
HALF = HEADS // 2
TOK = 256
D = 1024
NX, NY, NZ = 4, 8, 8
ZH = NZ // 2
CHIPS = 2 * NY
NCTX = 2 * CHIPS
F32, BF16 = jnp.float32, jnp.bfloat16
MESH = pl.DeviceIdType.MESH


def device(x, y, z, core):
    return (((z % 2) * NY + y) * 2 + core, x * ZH + z // 2)


def dot(left, right, dims):
    return lax.dot_general(left, right, (dims, ((), ())), preferred_element_type=F32)


def tn(left, right):
    return dot(left, right, ((0,), (0,)))


def nt(left, right):
    return dot(left, right, ((1,), (1,)))


def nn(left, right):
    return dot(left, right, ((1,), (0,)))


def head(h):
    return slice(h * HEAD, h * HEAD + HEAD)


def kernel(
    att_scale, inv_root,
    q_hbm, k_hbm, v_hbm, g_hbm, w_hbm,
    dq_ref, dk_ref, dv_ref, wg_ref,
    q, k, v, g, w, g_other, v_turned,
    tiles, weight, flat, to_rows, to_tiles,
    kv, kv_pair, kv_out, kv_in, kv_sum, kv_back, kv_give, state,
    qd, qd_pair, qd_out, qd_in, qd_sum, qd_back, qd_give, carried,
    scores, att_acc, att, att_in, att_grad, dk_acc, dv_acc,
    sum1, in1, sum2, in2, sum3, in3,
    in1a, in1b, sum2a, sum2b, in2a, in2b, sum3c, in3c,
    load_sem, ag_s, ag_r, pair_s, pair_r, scan_s, scan_r, rs_s, rs_r,
):
    ctx, dp = lax.axis_index("ctx"), lax.axis_index("dp")
    core, chip = ctx % 2, ctx // 2
    y, zl = chip % NY, chip // NY
    x, zh = dp // ZH, dp % ZH
    z = zh * 2 + zl
    mine, theirs = pl.ds(core * HALF, HALF), pl.ds((1 - core) * HALF, HALF)
    other = (chip * 2 + 1 - core, dp)

    def at_x(o):
        return device((x + o) % NX, y, z, core)

    def at_y(o):
        return device(x, (y + o) % NY, z, core)

    def at_z(o):
        return device(x, y, (z + o) % NZ, core)

    def remote(src, dst, s, r, to):
        return pltpu.make_async_remote_copy(
            src_ref=src, dst_ref=dst, send_sem=s, recv_sem=r, device_id=to, device_id_type=MESH
        )

    def by_core(of_core_0, of_core_1):
        pl.when(core == 0)(of_core_0)
        pl.when(core == 1)(of_core_1)

    sent, open_waits = [], {}

    def begin(name, make):
        for copy in make():
            copy.start()
        open_waits[name] = lambda: [copy.wait_recv() for copy in make()]
        sent.append(lambda: [copy.wait_send() for copy in make()])

    def begin_by_core(name, make_0, make_1):
        by_core(lambda: [copy.start() for copy in make_0()] and None, lambda: [copy.start() for copy in make_1()] and None)
        open_waits[name] = lambda: by_core(
            lambda: [copy.wait_recv() for copy in make_0()] and None,
            lambda: [copy.wait_recv() for copy in make_1()] and None,
        )
        sent.append(
            lambda: by_core(
                lambda: [copy.wait_send() for copy in make_0()] and None,
                lambda: [copy.wait_send() for copy in make_1()] and None,
            )
        )

    def wait(name):
        open_waits.pop(name)()

    loads = [
        pltpu.make_async_copy(src, dst, load_sem.at[i])
        for i, (src, dst) in enumerate(((k_hbm, k), (v_hbm, v), (w_hbm, w), (q_hbm, q), (g_hbm, g)))
    ]
    barrier = pltpu.get_barrier_semaphore()

    def enter():
        for load in loads:
            load.start()
        greeted = [((((chip + o) % CHIPS) * 2 + core), dp) for o in range(1, CHIPS)]
        greeted += [other]
        greeted += [at_x(o) for o in range(1, NX)]
        greeted += [
            device(x, y, (zh * 2 + 2 * (o // 2) + (zl + o) % 2) % NZ, core) for o in range(2, NZ)
        ]
        for to in greeted:
            pl.semaphore_signal(barrier, inc=1, device_id=to, device_id_type=MESH)
        loads[2].wait()
        own = w[...].astype(F32)
        for row in range(2):
            for cb in range(8):
                flat[row * 8 + cb : row * 8 + cb + 1, :] = own[row : row + 1, head(cb)]
        tiles[zl, y, core, x, zh] = flat[...].astype(BF16)
        pl.semaphore_wait(barrier, len(greeted))

    def products():
        loads[0].wait()
        loads[1].wait()
        for h in range(HEADS):
            turned = v[:, head(h)].T
            v_turned[head(h), :] = turned
            kv[h] = nn(turned, k[:, head(h)])

    def one_hot():
        rows_i = lax.broadcasted_iota(jnp.int32, (256, 256), 0)
        cols_i = lax.broadcasted_iota(jnp.int32, (256, 256), 1)

        def tile_row(i):
            return ((i & 31) >> 1) * 16 + (i & 1) * 8 + (i >> 5)

        to_rows[...] = jnp.where(cols_i == tile_row(rows_i), 1.0, 0.0).astype(BF16)
        to_tiles[...] = jnp.where(rows_i == tile_row(cols_i), 1.0, 0.0).astype(BF16)

    def ring(ref, first, to, n):
        return [remote(ref, ref, ag_s.at[first + o], ag_r.at[first + o], to(o)) for o in range(1, n)]

    def gather1_0():
        return ring(tiles.at[zl, y, 0, x, zh], 0, at_y, NY)

    def gather1_1():
        return ring(tiles.at[zl, y, 1, x, zh], 0, at_x, NX)

    def gather2_0():
        return ring(tiles.at[zl, :, 0, x, zh], 8, at_z, NZ)

    def gather2_1():
        return ring(tiles.at[zl, y, 1, 0:2, zh], 8, at_y, NY) + ring(tiles.at[zl, y, 1, 2:4, zh], 16, at_z, NZ)

    def gather3_0():
        return ring(tiles.at[:, :, 0, x], 24, at_x, NX)

    def gather3_1():
        return ring(tiles.at[zl, :, 1, 0:2, zh], 24, at_z, NZ) + ring(tiles.at[:, y, 1, 2:4], 32, at_y, NY)

    def swap_refs_0():
        return [tiles.at[:, :, 0, (x - o + NX) % NX] for o in range(NX)]

    def swap_refs_1():
        refs = []
        for o in range(NZ):
            far = (z - o + NZ) % NZ
            refs.append(tiles.at[far % 2, :, 1, 0:2, far // 2])
        return refs + [tiles.at[:, (y - o + NY) % NY, 1, 2:4] for o in range(NY)]

    def swap(refs):
        return [remote(ref, ref, ag_s.at[40 + i], ag_r.at[40 + i], other) for i, ref in enumerate(refs)]

    def hand_over():
        def go(arriving, refs, own):
            copies = swap(refs)
            for i in own:
                copies[i].start()
            for copy, i in arriving:
                copy.wait_recv()
                copies[i].start()

        def go_0():
            go(zip(gather3_0(), range(1, NX)), swap_refs_0(), [0])

        def go_1():
            order = list(zip(gather3_1(), list(range(1, NZ)) + list(range(NZ + 1, NZ + NY))))
            both = [p for pair in zip(order[: NZ - 1], order[NZ - 1 :]) for p in pair]
            go(both, swap_refs_1(), [0, NZ])

        open_waits.pop("gather3")
        by_core(go_0, go_1)
        open_waits["swap"] = lambda: by_core(
            lambda: [copy.wait_recv() for copy in swap(swap_refs_1())] and None,
            lambda: [copy.wait_recv() for copy in swap(swap_refs_0())] and None,
        )
        sent.append(
            lambda: by_core(
                lambda: [copy.wait_send() for copy in swap(swap_refs_0())] and None,
                lambda: [copy.wait_send() for copy in swap(swap_refs_1())] and None,
            )
        )

    def place(which):
        def one(b, carry):
            both = jnp.concatenate([tiles[a, b, which].reshape(256, 128) for a in range(2)], 1)
            rows = nn(to_rows[...], both).astype(BF16)
            for a in range(2):
                at = pl.ds(pl.multiple_of(((a * NY + b) * 2 + which) * 32, 32), 32)
                for cb in range(8):
                    weight[at, cb * 128 : cb * 128 + 128] = rows[cb * 32 : cb * 32 + 32, a * 128 : a * 128 + 128]
            return carry

        lax.fori_loop(0, NY, one, 0)

    def pair(src, dst, i):
        return lambda: [remote(src, dst, pair_s.at[i], pair_r.at[i], other)]

    def exchange(src, dst, i):
        def make():
            copies = []
            for o in range(1, CHIPS):
                to = (chip + o) % CHIPS
                copies.append(
                    remote(src.at[to], dst.at[chip], scan_s.at[i, o], scan_r.at[i, o], (to * 2 + core, dp))
                )
            return copies

        return make

    def add_pair(product, received, out):
        for h in range(HALF):
            both = product[core * HALF + h] + received[h]
            out[h * 4 : h * 4 + 4] = both.astype(BF16).reshape(4, 32, HEAD)

    def running(received, out, order):
        total = jnp.zeros((32, HEAD), F32)
        for s in order:
            out[s] = total.astype(BF16)
            total = total + received[s].astype(F32)

    def finish(product, received, back, give, out, core_behind):
        for h in range(HALF):
            base = back[h * 4 : h * 4 + 4].reshape(HEAD, HEAD).astype(F32)
            keep = jnp.where(core == core_behind, base + received[h], base)
            hand = jnp.where(core == core_behind, base, base + product[core * HALF + h])
            out[core * HALF + h] = keep.astype(BF16)
            give[h] = hand.astype(BF16)

    def spread(src, dst, first, to, n):
        return [remote(src(o), dst.at[o - 1], rs_s.at[first + o], rs_r.at[first + o], to(o)) for o in range(1, n)]

    def far_z(o):
        return (z + o) % NZ

    def far_y(o):
        return (y + o) % NY

    def scatter1_0(a, half):
        rows = pl.ds(half * 4, 4)
        copies = []
        for o in range(1, NX):
            i = (a * 2 + half) * NX + o
            copies.append(
                remote(
                    sum1.at[(x + o) % NX, :, a, rows], in1.at[o - 1, :, a, rows], rs_s.at[i], rs_r.at[i], at_x(o)
                )
            )
        return copies

    def scatter1_z(o, half):
        rows, far = pl.ds(half * 4, 4), (z + o) % NZ
        i = half * NZ + o
        return remote(
            sum1.at[0:2, far // 2, far % 2, rows], in1a.at[o - 1, :, rows], rs_s.at[i], rs_r.at[i], at_z(o)
        )

    def scatter1_y(o):
        i = 2 * NZ + o
        return remote(sum1.at[2:4, :, :, (y + o) % NY], in1b.at[o - 1], rs_s.at[i], rs_r.at[i], at_y(o))

    def scatter1(a, half):
        def of_core_0():
            for copy in scatter1_0(a, half):
                copy.start()

        def of_core_1():
            for far in range(ZH):
                o = (far * 2 + a - z + NZ) % NZ

                @pl.when(o != 0)
                def _():
                    scatter1_z(o, half).start()

            if a == 1:
                for far in range(4):
                    o = (half * 4 + far - y + NY) % NY

                    @pl.when(o != 0)
                    def _():
                        scatter1_y(o).start()

        by_core(of_core_0, of_core_1)

    def scatter1_all(act):
        def of_core_0():
            for half in range(2):
                for a in range(2):
                    for copy in scatter1_0(a, half):
                        act(copy)

        def of_core_1():
            for half in range(2):
                for o in range(1, NZ):
                    act(scatter1_z(o, half))
            for o in range(1, NY):
                act(scatter1_y(o))

        by_core(of_core_0, of_core_1)

    def scatter2_0():
        return spread(lambda o: sum2.at[far_z(o)], in2, 24, at_z, NZ)

    def scatter2_1():
        return spread(lambda o: sum2a.at[:, far_y(o)], in2a, 24, at_y, NY) + spread(
            lambda o: sum2b.at[:, far_z(o) // 2, far_z(o) % 2], in2b, 32, at_z, NZ
        )

    def scatter3_0():
        return spread(lambda o: sum3.at[far_y(o)], in3, 40, at_y, NY)

    def scatter3_1():
        return spread(lambda o: sum3c.at[(x + o) % NX], in3c, 40, at_x, NX)

    def total_of(own, received):
        value = own.astype(F32)
        for i in range(received.shape[0]):
            value = value + received[i].astype(F32)
        return value

    causal_t = lax.broadcasted_iota(jnp.int32, (TOK, TOK), 1) >= lax.broadcasted_iota(jnp.int32, (TOK, TOK), 0)

    def begin_all():
        begin_by_core("gather1", gather1_0, gather1_1)
        products()
        begin("kv pair", pair(kv.at[theirs], kv_pair, 0))
        loads[3].wait()
        loads[4].wait()
        begin("out_grad", pair(g, g_other, 1))
        one_hot()

    def kv_there():
        wait("kv pair")
        add_pair(kv, kv_pair, kv_out)
        begin("kv there", exchange(kv_out, kv_in, 0))
        kv_in[chip] = kv_out[chip]

    def second_gather():
        wait("gather1")
        begin_by_core("gather2", gather2_0, gather2_1)

    def score():
        for h in range(HEADS):
            masked = jnp.where(causal_t, nt(k[:, head(h)], q[:, head(h)]), 0.0).astype(BF16)
            scores[h] = masked
            att_acc[head(h), :] = nn(v_turned[head(h), :], masked)

    def third_gather():
        wait("gather2")
        begin_by_core("gather3", gather3_0, gather3_1)

    def kv_home():
        wait("kv there")
        running(kv_in, kv_sum, range(CHIPS))
        begin("kv home", exchange(kv_sum, kv_back, 1))
        kv_back[chip] = kv_sum[chip]

    def states():
        wait("kv home")
        finish(kv, kv_pair, kv_back, kv_give, state, 1)
        begin("states", pair(kv_give, state.at[mine], 2))

    def attend():
        wait("states")
        for h in range(HEADS):
            mixed = att_scale * (att_acc[head(h), :] + nt(state[h], q[:, head(h)]))
            att[2 * h : 2 * h + 2] = mixed.astype(BF16).reshape(2, 2, 32, TOK)
        begin("attended", pair(att.at[:, 1 - core], att_in, 3))

    def terms():
        wait("out_grad")
        wait("attended")
        for half, a in ((0, 0), (0, 1), (1, 0), (1, 1)):
            first = a * NY + half * 4
            blocks = slice(first, first + 4)
            left = att[blocks, core].reshape(128, TOK)
            right = att_in[blocks].reshape(128, TOK)
            term = (nn(left, g[...]) + nn(right, g_other[...])).astype(BF16)
            for j in range(2):
                both = jnp.concatenate(
                    [
                        jnp.concatenate(
                            [term[b * 32 : b * 32 + 32, head(cb)] for cb in range(8)], 0
                        )
                        for b in (2 * j, 2 * j + 1)
                    ],
                    1,
                )
                units = nn(to_tiles[...], both).astype(BF16)
                for b in range(2):
                    sum1[:, :, a, half * 4 + 2 * j + b] = units[:, head(b)].reshape(NX, ZH, 16, 128)
            scatter1(a, half)
        open_waits["scatter1"] = lambda: scatter1_all(lambda copy: copy.wait_recv())
        sent.append(lambda: scatter1_all(lambda copy: copy.wait_send()))

    def own_weights():
        place(core)

    def other_weights():
        wait("swap")
        place(1 - core)

    def qd_pairs():
        for i in range(4):
            rows = slice(i * 256, i * 256 + 256)
            grad = nt(weight[rows, :], g[...]).astype(BF16)
            att_grad[rows, :] = grad
            for h in range(2):
                qd[2 * i + h] = nn(grad[head(h)], q[:, head(2 * i + h)])
        begin("qd pair", pair(qd.at[theirs], qd_pair, 4))

    def qd_there():
        wait("qd pair")
        add_pair(qd, qd_pair, qd_out)
        begin("qd there", exchange(qd_out, qd_in, 2))
        qd_in[chip] = qd_out[chip]

    def local_grads():
        for h in range(HEADS):
            grad = att_grad[head(h), :]
            masked = jnp.where(causal_t, nn(v[:, head(h)], grad), 0.0).astype(BF16)
            dq_ref[:, head(h)] = (att_scale * (tn(masked, k[:, head(h)]) + tn(grad, state[h]))).astype(BF16)
            dk_acc[:, head(h)] = nn(masked, q[:, head(h)])
            dv_acc[:, head(h)] = nt(scores[h], grad)

    def second_scatter():
        wait("scatter1")

        def sum_0():
            def one(i, carry):
                value = sum1[x, i // 2, i % 2].astype(F32)
                for o in range(NX - 1):
                    value = value + in1[o, i // 2, i % 2].astype(F32)
                sum2[i] = value.astype(BF16)
                return carry

            lax.fori_loop(0, NZ, one, 0)

        def sum_1():
            sum2a[...] = total_of(sum1[0:2, zh, zl], in1a).astype(BF16)
            sum2b[...] = total_of(sum1[2:4, :, :, y], in1b).astype(BF16)

        by_core(sum_0, sum_1)
        begin_by_core("scatter2", scatter2_0, scatter2_1)

    def qd_home():
        wait("qd there")
        running(qd_in, qd_sum, reversed(range(CHIPS)))
        begin("qd home", exchange(qd_sum, qd_back, 3))
        qd_back[chip] = qd_sum[chip]

    def third_scatter():
        wait("scatter2")

        def sum_0():
            sum3[...] = total_of(sum2[z], in2)

        def sum_1():
            sum3c[0:2] = total_of(sum2a[:, y], in2a)
            sum3c[2:4] = total_of(sum2b[:, zh, zl], in2b)

        by_core(sum_0, sum_1)
        begin_by_core("scatter3", scatter3_0, scatter3_1)

    def laters():
        wait("qd home")
        finish(qd, qd_pair, qd_back, qd_give, carried, 0)
        begin("carried", pair(qd_give, carried.at[mine], 5))

    def weight_grad():
        wait("scatter3")

        def write(value):
            value = value * inv_root
            for row in range(2):
                for cb in range(8):
                    wg_ref[row : row + 1, head(cb)] = value[row * 8 + cb : row * 8 + cb + 1, :]

        by_core(lambda: write(total_of(sum3[y], in3)), lambda: write(total_of(sum3c[x], in3c)))

    def last_grads():
        wait("carried")
        for h in range(HEADS):
            dk_ref[:, head(h)] = (att_scale * (dk_acc[:, head(h)] + nn(v[:, head(h)], carried[h]))).astype(BF16)
            dv_ref[:, head(h)] = (att_scale * (dv_acc[:, head(h)] + nt(k[:, head(h)], carried[h]))).astype(BF16)

    steps = [
        enter, begin_all, kv_there, second_gather, score, third_gather, kv_home,
        hand_over, states, own_weights, attend, other_weights, qd_pairs, terms, qd_there, local_grads,
        second_scatter, qd_home, third_scatter, laters, weight_grad, last_grads,
    ]
    for step in steps:
        step()
    for name in list(open_waits):
        wait(name)
    for done in sent:
        done()


def store(*refs):
    sems = refs[8]
    copies = [pltpu.make_async_copy(refs[i], refs[4 + i], sems.at[i]) for i in range(4)]
    for copy in copies:
        copy.start()
    for copy in copies:
        copy.wait()


def per_device(queries, key_vecs, value_vecs, out_grad, out_weight):
    att_scale = 1.0 / math.sqrt(HEAD * TOK * NCTX)
    inv_root = 1.0 / math.sqrt(16 * TOK * NCTX)

    def body(*refs):
        kernel(att_scale, inv_root, *refs)

    hbm = pl.BlockSpec(memory_space=pltpu.HBM)
    vmem = pl.BlockSpec(memory_space=pltpu.VMEM)
    wide, narrow = pltpu.VMEM((TOK, D), F32), pltpu.VMEM((TOK, D), BF16)
    piece = pltpu.VMEM((CHIPS, 32, HEAD), BF16)
    scan = [
        pltpu.VMEM((HEADS, HEAD, HEAD), F32), pltpu.VMEM((HALF, HEAD, HEAD), F32),
        piece, piece, piece, piece,
        pltpu.VMEM((HALF, HEAD, HEAD), BF16), pltpu.VMEM((HEADS, HEAD, HEAD), BF16),
    ]
    unit = (16, 128)

    def units(*dims, kind=BF16):
        return pltpu.VMEM(dims + unit, kind)

    out = jax.ShapeDtypeStruct((TOK, D), BF16)
    dq, dk, dv, wg = pl.pallas_call(
        body,
        out_shape=(out, out, out, jax.ShapeDtypeStruct((2, D), F32)),
        in_specs=[hbm] * 5,
        out_specs=(vmem,) * 4,
        scratch_shapes=[
            narrow, narrow, narrow, narrow, pltpu.VMEM((2, D), BF16), narrow, pltpu.VMEM((D, TOK), BF16),
            units(2, NY, 2, NX, ZH), pltpu.VMEM((D, D), BF16), pltpu.VMEM(unit, F32),
            pltpu.VMEM((256, 256), BF16), pltpu.VMEM((256, 256), BF16),
            *scan, *scan,
            pltpu.VMEM((HEADS, TOK, TOK), BF16), pltpu.VMEM((D, TOK), F32),
            pltpu.VMEM((CHIPS, 2, 32, TOK), BF16), pltpu.VMEM((CHIPS, 32, TOK), BF16), pltpu.VMEM((D, TOK), BF16), wide, wide,
            units(NX, ZH, 2, NY), units(NX - 1, ZH, 2, NY),
            units(NZ, NY), units(NZ - 1, NY), units(NY, kind=F32), units(NY - 1, kind=F32),
            units(NZ - 1, 2, NY), units(NY - 1, 2, ZH, 2), units(2, NY), units(2, ZH, 2),
            units(NY - 1, 2), units(NZ - 1, 2), units(NX, kind=F32), units(NX - 1, kind=F32),
            pltpu.SemaphoreType.DMA((5,)),
            pltpu.SemaphoreType.DMA((56,)), pltpu.SemaphoreType.DMA((56,)),
            pltpu.SemaphoreType.DMA((6,)), pltpu.SemaphoreType.DMA((6,)),
            pltpu.SemaphoreType.DMA((4, CHIPS)), pltpu.SemaphoreType.DMA((4, CHIPS)),
            pltpu.SemaphoreType.DMA((48,)), pltpu.SemaphoreType.DMA((48,)),
        ],
        compiler_params=pltpu.CompilerParams(
            collective_id=0, has_side_effects=True, vmem_limit_bytes=(62 << 20) + (256 << 10)
        ),
        name="backward",
    )(queries[0], key_vecs[0], value_vecs[0], out_grad[0], out_weight)
    dq, dk, dv, wg = pl.pallas_call(
        store,
        out_shape=(out, out, out, jax.ShapeDtypeStruct((2, D), F32)),
        in_specs=[hbm] * 4,
        out_specs=(hbm,) * 4,
        scratch_shapes=[pltpu.SemaphoreType.DMA((4,))],
        name="store",
    )(dq, dk, dv, wg)
    return dq[None], dk[None], dv[None], wg


def solution(mesh):
    rows = P("dp", "ctx", None)
    return jax.shard_map(
        per_device,
        mesh=mesh,
        in_specs=(rows, rows, rows, rows, P(("ctx", "dp"), None)),
        out_specs=(rows, rows, rows, P(("ctx", "dp"), None)),
        check_vma=False,
    )
```

time: 1410 us -> 117 us (0.08)
  waiting for transfers between devices: 1310 us -> 0 us
  Pallas kernels: 0 us -> 116 us
  blocking collectives: 27 us -> 0 us
  starting transfers between devices: 20 us -> 0 us
  matrix products: 16.7 us -> 0 us
  local copies, waits for them, and re-layouts: 16.2 us -> 0 us
    all_gather x1 -> x0, waiting for transfers between devices: 1000 us -> none  [per_device(): lax.all_gather(out_weight, ('ctx', 'dp'), axis=0, tiled=True)]
    unnamed x3 -> x0, waiting for transfers between devices: 280 us -> none
    pallas_call x0 -> x2, Pallas kernels: none -> 116 us  [the longest x1 67.2 us: per_device(): pl.pallas_call(body, out_shape=(out, out, out, jax.ShapeDtypeStruct((2, D...]
    all_to_all x1 -> x0, blocking collectives: 27 us -> none  [per_device(): lax.all_to_all(local_kv.reshape(n_ctx, rows_each, HEAD), 'ctx', split_axi...]
    all_to_all x3 -> x0, waiting for transfers between devices: 23 us -> none  [the longest x1 12.7 us: per_device(): lax.all_to_all(kv_earlier, 'ctx', split_axis=0, concat_axis=0, tiled=True)]
    all_to_all x3 -> x0, starting transfers between devices: 19.9 us -> none  [the longest x1 7.44 us: per_device(): lax.all_to_all(qd_later, 'ctx', split_axis=0, concat_axis=0, tiled=True)]
    dot_general x14 -> x0, matrix products: 16.7 us -> none  [the longest x12 11.6 us: ein(): return jnp.einsum(form, left, right, preferred_element_type=jnp.float32)]
  transfers between devices with their start and end apart: 5 -> 0, of which waited for: 4 -> 0; matrix products, arithmetic and copies ran while one was open for 2% -> 0% of each run, Pallas kernels for 0% -> 0%
where the time goes in v2:
time: 117 us
  Pallas kernels  116 us (99%)
    pallas_call x1, Pallas kernels, per_device(): pl.pallas_call(body, out_shape=(out, out, out, jax.ShapeDtypeStruct((2, D...  67.2 us
    pallas_call x1, Pallas kernels, per_device(): pl.pallas_call(store, out_shape=(out, out, out, jax.ShapeDtypeStruct((2,...  49 us

profile of v2, /device:TPU:1, one launch (start us, length us, event | category | flops | bytes accessed | tf_op | source)
XLA Modules:
  0.0 116.9 jit_solution(15327885077799517998)
XLA Ops:
  0.6 67.2 %backward.1 = (bf16[256,1024]{1,0:T(8,128)(2,1)}, bf16[256,1024]{1,0:T(8,128)(2,1)}, bf16[256,1024]{1,0:T(8,128)(2,1)}, f32[2,1024]{1,0:T(2,128)}) custom-call(bf16[256,1024]{1,0:T(8,128)(2,1)} %bitcast.7, bf16[256,1024]{1,0:T(8,128)(2,1)} %bitcast.8, bf16[256,1024]{1,0:T(8,128)(2,1)} %bitcast.9, bf16[256,1024]{1,0:T(8,128)(2,1)} %bitcast.10, ...), custom_call_target="tpu_custom_call" | custom-call | tf_op jit(solution)/shard_map/backward/pallas_call | solution.py:564
  67.8 49.0 %store.1 = (bf16[256,1024]{1,0:T(8,128)(2,1)}, bf16[256,1024]{1,0:T(8,128)(2,1)}, bf16[256,1024]{1,0:T(8,128)(2,1)}, f32[2,1024]{1,0:T(2,128)}) custom-call(bf16[256,1024]{1,0:T(8,128)(2,1)} %get-tuple-element.12.refs_0_, bf16[256,1024]{1,0:T(8,128)(2,1)} %get-tuple-element.13.refs_1_, bf16[256,1024]{1,0:T(8,128)(2,1)} %get-tuple-element.14.refs_2_, ...), custom_call_target="tpu_custom_call" | custom-call | tf_op jit(solution)/shard_map/store/pallas_call | solution.py:591

commit v3 on v2

--- a/solution.py
+++ b/solution.py
@@ -48,7 +48,7 @@
     att_scale, inv_root,
     q_hbm, k_hbm, v_hbm, g_hbm, w_hbm,
     dq_ref, dk_ref, dv_ref, wg_ref,
-    q, k, v, g, w, g_other, v_turned,
+    q, k, v, g_both, w, v_turned,
     tiles, weight, flat, to_rows, to_tiles,
     kv, kv_pair, kv_out, kv_in, kv_sum, kv_back, kv_give, state,
     qd, qd_pair, qd_out, qd_in, qd_sum, qd_back, qd_give, carried,
@@ -106,6 +106,8 @@
 
     def wait(name):
         open_waits.pop(name)()
+
+    g, g_other = g_both.at[0:TOK], g_both.at[TOK : 2 * TOK]
 
     loads = [
         pltpu.make_async_copy(src, dst, load_sem.at[i])
@@ -292,12 +294,13 @@
         i = 2 * NZ + o
         return remote(sum1.at[2:4, :, :, (y + o) % NY], in1b.at[o - 1], rs_s.at[i], rs_r.at[i], at_y(o))
 
-    def scatter1(a, half):
+    def scatter1(turn):
         def of_core_0():
-            for copy in scatter1_0(a, half):
+            for copy in scatter1_0(turn // 2, turn % 2):
                 copy.start()
 
         def of_core_1():
+            a, half = turn % 2, turn // 2
             for far in range(ZH):
                 o = (far * 2 + a - z + NZ) % NZ
 
@@ -331,13 +334,32 @@
 
         by_core(of_core_0, of_core_1)
 
-    def scatter2_0():
-        return spread(lambda o: sum2.at[far_z(o)], in2, 24, at_z, NZ)
-
-    def scatter2_1():
-        return spread(lambda o: sum2a.at[:, far_y(o)], in2a, 24, at_y, NY) + spread(
-            lambda o: sum2b.at[:, far_z(o) // 2, far_z(o) % 2], in2b, 32, at_z, NZ
+    def scatter2_z0(o):
+        far = (z + o) % NZ
+        return remote(sum2.at[far], in2.at[o - 1], rs_s.at[24 + o], rs_r.at[24 + o], at_z(o))
+
+    def scatter2_y1(o):
+        far = (y + o) % NY
+        return remote(sum2a.at[:, far], in2a.at[o - 1], rs_s.at[24 + o], rs_r.at[24 + o], at_y(o))
+
+    def scatter2_z1(o):
+        far = (z + o) % NZ
+        return remote(
+            sum2b.at[:, far // 2, far % 2], in2b.at[o - 1], rs_s.at[32 + o], rs_r.at[32 + o], at_z(o)
         )
+
+    def scatter2_all(act):
+        def of_core_0():
+            for o in range(1, NZ):
+                act(scatter2_z0(o))
+
+        def of_core_1():
+            for o in range(1, NY):
+                act(scatter2_y1(o))
+            for o in range(1, NZ):
+                act(scatter2_z1(o))
+
+        by_core(of_core_0, of_core_1)
 
     def scatter3_0():
         return spread(lambda o: sum3.at[far_y(o)], in3, 40, at_y, NY)
@@ -403,12 +425,14 @@
     def terms():
         wait("out_grad")
         wait("attended")
-        for half, a in ((0, 0), (0, 1), (1, 0), (1, 1)):
-            first = a * NY + half * 4
-            blocks = slice(first, first + 4)
-            left = att[blocks, core].reshape(128, TOK)
-            right = att_in[blocks].reshape(128, TOK)
-            term = (nn(left, g[...]) + nn(right, g_other[...])).astype(BF16)
+        for turn in range(4):
+            a = (1 - core) * (turn // 2) + core * (turn % 2)
+            half = (1 - core) * (turn % 2) + core * (turn // 2)
+            blocks = pl.ds(a * NY + half * 4, 4)
+            left = jnp.concatenate(
+                [att[blocks, core].reshape(128, TOK), att_in[blocks].reshape(128, TOK)], 1
+            )
+            term = nn(left, g_both[...]).astype(BF16)
             for j in range(2):
                 both = jnp.concatenate(
                     [
@@ -422,8 +446,7 @@
                 units = nn(to_tiles[...], both).astype(BF16)
                 for b in range(2):
                     sum1[:, :, a, half * 4 + 2 * j + b] = units[:, head(b)].reshape(NX, ZH, 16, 128)
-            scatter1(a, half)
-        open_waits["scatter1"] = lambda: scatter1_all(lambda copy: copy.wait_recv())
+            scatter1(turn)
         sent.append(lambda: scatter1_all(lambda copy: copy.wait_send()))
 
     def own_weights():
@@ -434,13 +457,18 @@
         place(1 - core)
 
     def qd_pairs():
-        for i in range(4):
-            rows = slice(i * 256, i * 256 + 256)
-            grad = nt(weight[rows, :], g[...]).astype(BF16)
-            att_grad[rows, :] = grad
-            for h in range(2):
-                qd[2 * i + h] = nn(grad[head(h)], q[:, head(2 * i + h)])
+        def of_half(which):
+            for i in range(2):
+                rows = pl.ds(pl.multiple_of((which * 2 + i) * 256, 256), 256)
+                grad = nt(weight[rows, :], g[...]).astype(BF16)
+                att_grad[rows, :] = grad
+                for j in range(2):
+                    h = which * HALF + 2 * i + j
+                    qd[h] = nn(grad[head(j)], q[:, pl.ds(pl.multiple_of(h * HEAD, HEAD), HEAD)])
+
+        of_half(1 - core)
         begin("qd pair", pair(qd.at[theirs], qd_pair, 4))
+        of_half(core)
 
     def qd_there():
         wait("qd pair")
@@ -456,25 +484,54 @@
             dk_acc[:, head(h)] = nn(masked, q[:, head(h)])
             dv_acc[:, head(h)] = nt(scores[h], grad)
 
-    def second_scatter():
-        wait("scatter1")
-
-        def sum_0():
-            def one(i, carry):
-                value = sum1[x, i // 2, i % 2].astype(F32)
+    def second_scatter(part):
+        def of_core_0():
+            for half in range(2):
+                for copy in scatter1_0(part, half):
+                    copy.wait_recv()
+            for far in range(ZH):
+                value = sum1[x, far, part].astype(F32)
                 for o in range(NX - 1):
-                    value = value + in1[o, i // 2, i % 2].astype(F32)
-                sum2[i] = value.astype(BF16)
-                return carry
-
-            lax.fori_loop(0, NZ, one, 0)
-
-        def sum_1():
-            sum2a[...] = total_of(sum1[0:2, zh, zl], in1a).astype(BF16)
-            sum2b[...] = total_of(sum1[2:4, :, :, y], in1b).astype(BF16)
-
-        by_core(sum_0, sum_1)
-        begin_by_core("scatter2", scatter2_0, scatter2_1)
+                    value = value + in1[o, far, part].astype(F32)
+                sum2[far * 2 + part] = value.astype(BF16)
+                o = (far * 2 + part - z + NZ) % NZ
+
+                @pl.when(o != 0)
+                def _():
+                    scatter2_z0(o).start()
+
+        def of_core_1():
+            rows = slice(part * 4, part * 4 + 4)
+            for o in range(1, NZ):
+                scatter1_z(o, part).wait_recv()
+            value = sum1[0:2, zh, zl, rows].astype(F32)
+            for o in range(NZ - 1):
+                value = value + in1a[o, :, rows].astype(F32)
+            sum2a[:, rows] = value.astype(BF16)
+            for far in range(4):
+                o = (part * 4 + far - y + NY) % NY
+
+                @pl.when(o != 0)
+                def _():
+                    scatter2_y1(o).start()
+
+            if part == 1:
+                for o in range(1, NY):
+                    scatter1_y(o).wait_recv()
+                sum2b[...] = total_of(sum1[2:4, :, :, y], in1b).astype(BF16)
+                for o in range(1, NZ):
+                    scatter2_z1(o).start()
+
+        by_core(of_core_0, of_core_1)
+        if part == 1:
+            open_waits["scatter2"] = lambda: scatter2_all(lambda copy: copy.wait_recv())
+            sent.append(lambda: scatter2_all(lambda copy: copy.wait_send()))
+
+    def second_scatter_0():
+        second_scatter(0)
+
+    def second_scatter_1():
+        second_scatter(1)
 
     def qd_home():
         wait("qd there")
@@ -519,8 +576,8 @@
 
     steps = [
         enter, begin_all, kv_there, second_gather, score, third_gather, kv_home,
-        hand_over, states, own_weights, attend, other_weights, qd_pairs, terms, qd_there, local_grads,
-        second_scatter, qd_home, third_scatter, laters, weight_grad, last_grads,
+        hand_over, states, own_weights, attend, other_weights, qd_pairs, qd_there, terms, local_grads,
+        second_scatter_0, second_scatter_1, qd_home, third_scatter, laters, weight_grad, last_grads,
     ]
     for step in steps:
         step()
@@ -567,7 +624,7 @@
         in_specs=[hbm] * 5,
         out_specs=(vmem,) * 4,
         scratch_shapes=[
-            narrow, narrow, narrow, narrow, pltpu.VMEM((2, D), BF16), narrow, pltpu.VMEM((D, TOK), BF16),
+            narrow, narrow, narrow, pltpu.VMEM((2 * TOK, D), BF16), pltpu.VMEM((2, D), BF16), pltpu.VMEM((D, TOK), BF16),
             units(2, NY, 2, NX, ZH), pltpu.VMEM((D, D), BF16), pltpu.VMEM(unit, F32),
             pltpu.VMEM((256, 256), BF16), pltpu.VMEM((256, 256), BF16),
             *scan, *scan,
@@ -584,18 +641,18 @@
             pltpu.SemaphoreType.DMA((48,)), pltpu.SemaphoreType.DMA((48,)),
         ],
         compiler_params=pltpu.CompilerParams(
-            collective_id=0, has_side_effects=True, vmem_limit_bytes=(62 << 20) + (256 << 10)
+            collective_id=0, has_side_effects=True, vmem_limit_bytes=48 << 20
         ),
         name="backward",
-    )(queries[0], key_vecs[0], value_vecs[0], out_grad[0], out_weight)
+    )(*(pltpu.with_memory_space_constraint(a, pltpu.HBM) for a in (queries[0], key_vecs[0], value_vecs[0], out_grad[0], out_weight)))
     dq, dk, dv, wg = pl.pallas_call(
         store,
         out_shape=(out, out, out, jax.ShapeDtypeStruct((2, D), F32)),
-        in_specs=[hbm] * 4,
+        in_specs=[vmem] * 4,
         out_specs=(hbm,) * 4,
         scratch_shapes=[pltpu.SemaphoreType.DMA((4,))],
         name="store",
-    )(dq, dk, dv, wg)
+    )(*(pltpu.with_memory_space_constraint(a, pltpu.VMEM) for a in (dq, dk, dv, wg)))
     return dq[None], dk[None], dv[None], wg
 
 

time: 117 us -> 66.4 us (0.57)
  Pallas kernels: 116 us -> 65.7 us
    pallas_call x1, Pallas kernels: 49 us -> 1.18 us  [per_device(): pl.pallas_call(store, out_shape=(out, out, out, jax.ShapeDtypeStruct((2,...]
    pallas_call x1, Pallas kernels: 67.2 us -> 64.5 us  [per_device(): pl.pallas_call(body, out_shape=(out, out, out, jax.ShapeDtypeStruct((2, D...]
where the time goes in v3:
time: 66.4 us; the launch traced here: 66.3 us
  Pallas kernels  65.7 us (99%)
    pallas_call x1, Pallas kernels, per_device(): pl.pallas_call(body, out_shape=(out, out, out, jax.ShapeDtypeStruct((2, D...  64.5 us

profile of v3, /device:TPU:1, one launch (start us, length us, event | category | flops | bytes accessed | tf_op | source)
XLA Modules:
  0.0 66.3 jit_solution(17636653775434895143)
XLA Ops:
  0.6 64.5 %backward.1 = (bf16[256,1024]{1,0:T(8,128)(2,1)S(1)}, bf16[256,1024]{1,0:T(8,128)(2,1)S(1)}, bf16[256,1024]{1,0:T(8,128)(2,1)S(1)}, f32[2,1024]{1,0:T(2,128)S(1)}) custom-call(bf16[256,1024]{1,0:T(8,128)(2,1)} %bitcast.7, bf16[256,1024]{1,0:T(8,128)(2,1)} %bitcast.8, bf16[256,1024]{1,0:T(8,128)(2,1)} %bitcast.9, bf16[256,1024]{1,0:T(8,128)(2,1)} %bitcast.10, ...), custom_call_target="tpu_custom_call" | custom-call | tf_op jit(solution)/shard_map/backward/pallas_call | solution.py:621
  65.1 1.2 %store.1 = (bf16[256,1024]{1,0:T(8,128)(2,1)}, bf16[256,1024]{1,0:T(8,128)(2,1)}, bf16[256,1024]{1,0:T(8,128)(2,1)}, f32[2,1024]{1,0:T(2,128)}) custom-call(bf16[256,1024]{1,0:T(8,128)(2,1)S(1)} %get-tuple-element.12.refs_0_, bf16[256,1024]{1,0:T(8,128)(2,1)S(1)} %get-tuple-element.13.refs_1_, bf16[256,1024]{1,0:T(8,128)(2,1)S(1)} %get-tuple-element.14.refs_2_, ...), custom_call_target="tpu_custom_call" | custom-call | tf_op jit(solution)/shard_map/store/pallas_call | solution.py:648

commit v4 on v3

--- a/solution.py
+++ b/solution.py
@@ -48,11 +48,11 @@
     att_scale, inv_root,
     q_hbm, k_hbm, v_hbm, g_hbm, w_hbm,
     dq_ref, dk_ref, dv_ref, wg_ref,
-    q, k, v, g_both, w, v_turned,
+    q, k, v, g_both, w, v_turned, q_other,
     tiles, weight, flat, to_rows, to_tiles,
     kv, kv_pair, kv_out, kv_in, kv_sum, kv_back, kv_give, state,
-    qd, qd_pair, qd_out, qd_in, qd_sum, qd_back, qd_give, carried,
-    scores, att_acc, att, att_in, att_grad, dk_acc, dv_acc,
+    qd_own, qd_other, qd_out, qd_in, qd_sum, qd_back, qd_give, carried,
+    scores, att_acc, att, att_in, att_grad, grad_give, dk_acc, dv_acc,
     sum1, in1, sum2, in2, sum3, in3,
     in1a, in1b, sum2a, sum2b, in2a, in2b, sum3c, in3c,
     load_sem, ag_s, ag_r, pair_s, pair_r, scan_s, scan_r, rs_s, rs_r,
@@ -111,7 +111,7 @@
 
     loads = [
         pltpu.make_async_copy(src, dst, load_sem.at[i])
-        for i, (src, dst) in enumerate(((k_hbm, k), (v_hbm, v), (w_hbm, w), (q_hbm, q), (g_hbm, g)))
+        for i, (src, dst) in enumerate(((w_hbm, w), (k_hbm, k), (v_hbm, v), (q_hbm, q), (g_hbm, g)))
     ]
     barrier = pltpu.get_barrier_semaphore()
 
@@ -126,7 +126,7 @@
         ]
         for to in greeted:
             pl.semaphore_signal(barrier, inc=1, device_id=to, device_id_type=MESH)
-        loads[2].wait()
+        loads[0].wait()
         own = w[...].astype(F32)
         for row in range(2):
             for cb in range(8):
@@ -134,13 +134,13 @@
         tiles[zl, y, core, x, zh] = flat[...].astype(BF16)
         pl.semaphore_wait(barrier, len(greeted))
 
-    def products():
-        loads[0].wait()
-        loads[1].wait()
-        for h in range(HEADS):
-            turned = v[:, head(h)].T
-            v_turned[head(h), :] = turned
-            kv[h] = nn(turned, k[:, head(h)])
+    def products(which):
+        for i in range(HALF):
+            h = which * HALF + i
+            cols = pl.ds(pl.multiple_of(h * HEAD, HEAD), HEAD)
+            turned = v[:, cols].T
+            v_turned[cols, :] = turned
+            kv[h] = nn(turned, k[:, cols])
 
     def one_hot():
         rows_i = lax.broadcasted_iota(jnp.int32, (256, 256), 0)
@@ -164,69 +164,81 @@
     def gather2_0():
         return ring(tiles.at[zl, :, 0, x, zh], 8, at_z, NZ)
 
-    def gather2_1():
-        return ring(tiles.at[zl, y, 1, 0:2, zh], 8, at_y, NY) + ring(tiles.at[zl, y, 1, 2:4, zh], 16, at_z, NZ)
-
-    def gather3_0():
-        return ring(tiles.at[:, :, 0, x], 24, at_x, NX)
-
-    def gather3_1():
-        return ring(tiles.at[zl, :, 1, 0:2, zh], 24, at_z, NZ) + ring(tiles.at[:, y, 1, 2:4], 32, at_y, NY)
-
-    def swap_refs_0():
-        return [tiles.at[:, :, 0, (x - o + NX) % NX] for o in range(NX)]
-
-    def swap_refs_1():
-        refs = []
-        for o in range(NZ):
-            far = (z - o + NZ) % NZ
-            refs.append(tiles.at[far % 2, :, 1, 0:2, far // 2])
-        return refs + [tiles.at[:, (y - o + NY) % NY, 1, 2:4] for o in range(NY)]
-
-    def swap(refs):
-        return [remote(ref, ref, ag_s.at[40 + i], ag_r.at[40 + i], other) for i, ref in enumerate(refs)]
-
-    def hand_over():
-        def go(arriving, refs, own):
-            copies = swap(refs)
-            for i in own:
-                copies[i].start()
-            for copy, i in arriving:
+    def gather2_1y():
+        return ring(tiles.at[zl, y, 1, 0:2, zh], 8, at_y, NY)
+
+    def gather2_1z():
+        return ring(tiles.at[zl, y, 1, 2:4, zh], 16, at_z, NZ)
+
+    def gather3_0(o):
+        far = (z - o + NZ) % NZ
+        return ring(tiles.at[far % 2, :, 0, x, far // 2], 24 + o * NX, at_x, NX)
+
+    def gather3_1z():
+        return ring(tiles.at[zl, :, 1, 0:2, zh], 24, at_z, NZ)
+
+    def gather3_1y():
+        return ring(tiles.at[:, y, 1, 2:4], 32, at_y, NY)
+
+    def gather3_0_all():
+        return [copy for o in range(NZ) for copy in gather3_0(o)]
+
+    def start(copies):
+        for copy in copies:
+            copy.start()
+
+    def second_gather():
+        wait("gather1")
+
+        def of_core_0():
+            start(gather2_0())
+            start(gather3_0(0))
+
+        def of_core_1():
+            start(gather2_1y())
+            start(gather2_1z())
+
+        by_core(of_core_0, of_core_1)
+
+    def third_gather():
+        def of_core_0():
+            copies = gather2_0()
+            for o in (1, 7, 2, 6, 3, 5, 4):
+                copies[o - 1].wait_recv()
+                start(gather3_0(o))
+
+        def of_core_1():
+            for copy in gather2_1y():
                 copy.wait_recv()
-                copies[i].start()
-
-        def go_0():
-            go(zip(gather3_0(), range(1, NX)), swap_refs_0(), [0])
-
-        def go_1():
-            order = list(zip(gather3_1(), list(range(1, NZ)) + list(range(NZ + 1, NZ + NY))))
-            both = [p for pair in zip(order[: NZ - 1], order[NZ - 1 :]) for p in pair]
-            go(both, swap_refs_1(), [0, NZ])
-
-        open_waits.pop("gather3")
-        by_core(go_0, go_1)
-        open_waits["swap"] = lambda: by_core(
-            lambda: [copy.wait_recv() for copy in swap(swap_refs_1())] and None,
-            lambda: [copy.wait_recv() for copy in swap(swap_refs_0())] and None,
-        )
-        sent.append(
-            lambda: by_core(
-                lambda: [copy.wait_send() for copy in swap(swap_refs_0())] and None,
-                lambda: [copy.wait_send() for copy in swap(swap_refs_1())] and None,
-            )
-        )
-
-    def place(which):
-        def one(b, carry):
-            both = jnp.concatenate([tiles[a, b, which].reshape(256, 128) for a in range(2)], 1)
+            start(gather3_1z())
+            for copy in gather2_1z():
+                copy.wait_recv()
+            start(gather3_1y())
+
+        by_core(of_core_0, of_core_1)
+
+        def all_of(last_only, act):
+            def of_core_0():
+                for copy in gather3_0_all() + ([] if last_only else gather2_0()):
+                    act(copy)
+
+            def of_core_1():
+                for copy in gather3_1z() + gather3_1y() + ([] if last_only else gather2_1y() + gather2_1z()):
+                    act(copy)
+
+            by_core(of_core_0, of_core_1)
+
+        open_waits["gather3"] = lambda: all_of(True, lambda copy: copy.wait_recv())
+        sent.append(lambda: all_of(False, lambda copy: copy.wait_send()))
+
+    def place():
+        for b in range(NY):
+            both = jnp.concatenate([tiles[a, b, core].reshape(256, 128) for a in range(2)], 1)
             rows = nn(to_rows[...], both).astype(BF16)
             for a in range(2):
-                at = pl.ds(pl.multiple_of(((a * NY + b) * 2 + which) * 32, 32), 32)
+                at = (a * NY + b) * 32
                 for cb in range(8):
-                    weight[at, cb * 128 : cb * 128 + 128] = rows[cb * 32 : cb * 32 + 32, a * 128 : a * 128 + 128]
-            return carry
-
-        lax.fori_loop(0, NY, one, 0)
+                    weight[at : at + 32, head(cb)] = rows[cb * 32 : cb * 32 + 32, head(a)]
 
     def pair(src, dst, i):
         return lambda: [remote(src, dst, pair_s.at[i], pair_r.at[i], other)]
@@ -254,13 +266,11 @@
             out[s] = total.astype(BF16)
             total = total + received[s].astype(F32)
 
-    def finish(product, received, back, give, out, core_behind):
+    def finish():
         for h in range(HALF):
-            base = back[h * 4 : h * 4 + 4].reshape(HEAD, HEAD).astype(F32)
-            keep = jnp.where(core == core_behind, base + received[h], base)
-            hand = jnp.where(core == core_behind, base, base + product[core * HALF + h])
-            out[core * HALF + h] = keep.astype(BF16)
-            give[h] = hand.astype(BF16)
+            base = kv_back[h * 4 : h * 4 + 4].reshape(HEAD, HEAD).astype(F32)
+            state[core * HALF + h] = jnp.where(core == 1, base + kv_pair[h], base).astype(BF16)
+            kv_give[h] = jnp.where(core == 1, base, base + kv[core * HALF + h]).astype(BF16)
 
     def spread(src, dst, first, to, n):
         return [remote(src(o), dst.at[o - 1], rs_s.at[first + o], rs_r.at[first + o], to(o)) for o in range(1, n)]
@@ -377,12 +387,15 @@
 
     def begin_all():
         begin_by_core("gather1", gather1_0, gather1_1)
-        products()
+        loads[1].wait()
+        loads[2].wait()
+        products(1 - core)
         begin("kv pair", pair(kv.at[theirs], kv_pair, 0))
+        products(core)
         loads[3].wait()
         loads[4].wait()
         begin("out_grad", pair(g, g_other, 1))
-        one_hot()
+        begin("queries", pair(q, q_other, 4))
 
     def kv_there():
         wait("kv pair")
@@ -390,29 +403,22 @@
         begin("kv there", exchange(kv_out, kv_in, 0))
         kv_in[chip] = kv_out[chip]
 
-    def second_gather():
-        wait("gather1")
-        begin_by_core("gather2", gather2_0, gather2_1)
-
     def score():
         for h in range(HEADS):
             masked = jnp.where(causal_t, nt(k[:, head(h)], q[:, head(h)]), 0.0).astype(BF16)
             scores[h] = masked
             att_acc[head(h), :] = nn(v_turned[head(h), :], masked)
 
-    def third_gather():
-        wait("gather2")
-        begin_by_core("gather3", gather3_0, gather3_1)
-
     def kv_home():
         wait("kv there")
         running(kv_in, kv_sum, range(CHIPS))
         begin("kv home", exchange(kv_sum, kv_back, 1))
         kv_back[chip] = kv_sum[chip]
+        one_hot()
 
     def states():
         wait("kv home")
-        finish(kv, kv_pair, kv_back, kv_give, state, 1)
+        finish()
         begin("states", pair(kv_give, state.at[mine], 2))
 
     def attend():
@@ -422,10 +428,17 @@
             att[2 * h : 2 * h + 2] = mixed.astype(BF16).reshape(2, 2, 32, TOK)
         begin("attended", pair(att.at[:, 1 - core], att_in, 3))
 
-    def terms():
+    def terms_0():
         wait("out_grad")
         wait("attended")
-        for turn in range(4):
+        terms((0, 1))
+
+    def terms_1():
+        terms((2, 3))
+        sent.append(lambda: scatter1_all(lambda copy: copy.wait_send()))
+
+    def terms(turns):
+        for turn in turns:
             a = (1 - core) * (turn // 2) + core * (turn % 2)
             half = (1 - core) * (turn % 2) + core * (turn // 2)
             blocks = pl.ds(a * NY + half * 4, 4)
@@ -447,38 +460,35 @@
                 for b in range(2):
                     sum1[:, :, a, half * 4 + 2 * j + b] = units[:, head(b)].reshape(NX, ZH, 16, 128)
             scatter1(turn)
-        sent.append(lambda: scatter1_all(lambda copy: copy.wait_send()))
-
-    def own_weights():
-        place(core)
-
-    def other_weights():
-        wait("swap")
-        place(1 - core)
-
-    def qd_pairs():
-        def of_half(which):
-            for i in range(2):
-                rows = pl.ds(pl.multiple_of((which * 2 + i) * 256, 256), 256)
-                grad = nt(weight[rows, :], g[...]).astype(BF16)
-                att_grad[rows, :] = grad
-                for j in range(2):
-                    h = which * HALF + 2 * i + j
-                    qd[h] = nn(grad[head(j)], q[:, pl.ds(pl.multiple_of(h * HEAD, HEAD), HEAD)])
-
-        of_half(1 - core)
-        begin("qd pair", pair(qd.at[theirs], qd_pair, 4))
-        of_half(core)
-
-    def qd_there():
-        wait("qd pair")
-        add_pair(qd, qd_pair, qd_out)
+
+
+    def att_grads():
+        wait("gather3")
+        place()
+        wait("queries")
+        for i in range(2):
+            at = slice(i * 8, i * 8 + 8)
+            grad = nt(weight[i * 256 : i * 256 + 256, :], g_both[...]).astype(BF16)
+            att_grad[at, core] = grad[:, :TOK].reshape(8, 32, TOK)
+            grad_give[at] = grad[:, TOK:].reshape(8, 32, TOK)
+            for j in range(4):
+                h, rows = i * 4 + j, slice(j * 64, j * 64 + 64)
+                here = nn(grad[rows, :TOK], q[:, head(h)])
+                there = nn(grad[rows, TOK:], q_other[:, head(h)])
+                qd_own[2 * h : 2 * h + 2] = here.reshape(2, 32, HEAD)
+                qd_other[2 * h : 2 * h + 2] = there.reshape(2, 32, HEAD)
+                qd_out[2 * h : 2 * h + 2] = (here + there).astype(BF16).reshape(2, 32, HEAD)
         begin("qd there", exchange(qd_out, qd_in, 2))
         qd_in[chip] = qd_out[chip]
+        for i in range(2):
+            at = slice(i * 8, i * 8 + 8)
+            begin(f"grad {i}", pair(grad_give.at[at], att_grad.at[at, core], 6 + i))
 
     def local_grads():
+        wait("grad 0")
+        wait("grad 1")
         for h in range(HEADS):
-            grad = att_grad[head(h), :]
+            grad = att_grad[2 * h : 2 * h + 2].reshape(HEAD, TOK)
             masked = jnp.where(causal_t, nn(v[:, head(h)], grad), 0.0).astype(BF16)
             dq_ref[:, head(h)] = (att_scale * (tn(masked, k[:, head(h)]) + tn(grad, state[h]))).astype(BF16)
             dk_acc[:, head(h)] = nn(masked, q[:, head(h)])
@@ -554,8 +564,10 @@
 
     def laters():
         wait("qd home")
-        finish(qd, qd_pair, qd_back, qd_give, carried, 0)
-        begin("carried", pair(qd_give, carried.at[mine], 5))
+        base = qd_back[...].astype(F32)
+        carried[:, core] = jnp.where(core == 0, base + qd_other[...], base).astype(BF16)
+        qd_give[...] = jnp.where(core == 0, base, base + qd_own[...]).astype(BF16)
+        begin("carried", pair(qd_give, carried.at[:, core], 5))
 
     def weight_grad():
         wait("scatter3")
@@ -571,12 +583,13 @@
     def last_grads():
         wait("carried")
         for h in range(HEADS):
-            dk_ref[:, head(h)] = (att_scale * (dk_acc[:, head(h)] + nn(v[:, head(h)], carried[h]))).astype(BF16)
-            dv_ref[:, head(h)] = (att_scale * (dv_acc[:, head(h)] + nt(k[:, head(h)], carried[h]))).astype(BF16)
+            later = carried[2 * h : 2 * h + 2].reshape(HEAD, HEAD)
+            dk_ref[:, head(h)] = (att_scale * (dk_acc[:, head(h)] + nn(v[:, head(h)], later))).astype(BF16)
+            dv_ref[:, head(h)] = (att_scale * (dv_acc[:, head(h)] + nt(k[:, head(h)], later))).astype(BF16)
 
     steps = [
-        enter, begin_all, kv_there, second_gather, score, third_gather, kv_home,
-        hand_over, states, own_weights, attend, other_weights, qd_pairs, qd_there, terms, local_grads,
+        enter, begin_all, kv_there, second_gather, score, kv_home, third_gather, states,
+        attend, terms_0, terms_1, att_grads, local_grads,
         second_scatter_0, second_scatter_1, qd_home, third_scatter, laters, weight_grad, last_grads,
     ]
     for step in steps:
@@ -624,19 +637,22 @@
         in_specs=[hbm] * 5,
         out_specs=(vmem,) * 4,
         scratch_shapes=[
-            narrow, narrow, narrow, pltpu.VMEM((2 * TOK, D), BF16), pltpu.VMEM((2, D), BF16), pltpu.VMEM((D, TOK), BF16),
-            units(2, NY, 2, NX, ZH), pltpu.VMEM((D, D), BF16), pltpu.VMEM(unit, F32),
+            narrow, narrow, narrow, pltpu.VMEM((2 * TOK, D), BF16), pltpu.VMEM((2, D), BF16), pltpu.VMEM((D, TOK), BF16), narrow,
+            units(2, NY, 2, NX, ZH), pltpu.VMEM((D // 2, D), BF16), pltpu.VMEM(unit, F32),
             pltpu.VMEM((256, 256), BF16), pltpu.VMEM((256, 256), BF16),
-            *scan, *scan,
+            *scan,
+            pltpu.VMEM((CHIPS, 32, HEAD), F32), pltpu.VMEM((CHIPS, 32, HEAD), F32),
+            piece, piece, piece, piece, piece, pltpu.VMEM((CHIPS, 2, 32, HEAD), BF16),
             pltpu.VMEM((HEADS, TOK, TOK), BF16), pltpu.VMEM((D, TOK), F32),
-            pltpu.VMEM((CHIPS, 2, 32, TOK), BF16), pltpu.VMEM((CHIPS, 32, TOK), BF16), pltpu.VMEM((D, TOK), BF16), wide, wide,
+            pltpu.VMEM((CHIPS, 2, 32, TOK), BF16), pltpu.VMEM((CHIPS, 32, TOK), BF16),
+            pltpu.VMEM((CHIPS, 2, 32, TOK), BF16), pltpu.VMEM((CHIPS, 32, TOK), BF16), wide, wide,
             units(NX, ZH, 2, NY), units(NX - 1, ZH, 2, NY),
             units(NZ, NY), units(NZ - 1, NY), units(NY, kind=F32), units(NY - 1, kind=F32),
             units(NZ - 1, 2, NY), units(NY - 1, 2, ZH, 2), units(2, NY), units(2, ZH, 2),
             units(NY - 1, 2), units(NZ - 1, 2), units(NX, kind=F32), units(NX - 1, kind=F32),
             pltpu.SemaphoreType.DMA((5,)),
             pltpu.SemaphoreType.DMA((56,)), pltpu.SemaphoreType.DMA((56,)),
-            pltpu.SemaphoreType.DMA((6,)), pltpu.SemaphoreType.DMA((6,)),
+            pltpu.SemaphoreType.DMA((8,)), pltpu.SemaphoreType.DMA((8,)),
             pltpu.SemaphoreType.DMA((4, CHIPS)), pltpu.SemaphoreType.DMA((4, CHIPS)),
             pltpu.SemaphoreType.DMA((48,)), pltpu.SemaphoreType.DMA((48,)),
         ],

time: 66.4 us -> 58.6 us (0.88)
  Pallas kernels: 65.7 us -> 57.8 us
    pallas_call x1, Pallas kernels: 64.5 us -> 56.7 us  [per_device(): pl.pallas_call(body, out_shape=(out, out, out, jax.ShapeDtypeStruct((2, D...]
where the time goes in v4:
time: 58.6 us; the launch traced here: 58.5 us
  Pallas kernels  57.8 us (99%)
  between operations  0.64 us (1%)
    pallas_call x1, Pallas kernels, per_device(): pl.pallas_call(body, out_shape=(out, out, out, jax.ShapeDtypeStruct((2, D...  56.7 us
    pallas_call x1, Pallas kernels, per_device(): pl.pallas_call(store, out_shape=(out, out, out, jax.ShapeDtypeStruct((2,...  1.18 us

profile of v4, /device:TPU:1, one launch (start us, length us, event | category | flops | bytes accessed | tf_op | source)
XLA Modules:
  0.0 58.5 jit_solution(13148646690369106143)
XLA Ops:
  0.6 56.7 %backward.1 = (bf16[256,1024]{1,0:T(8,128)(2,1)S(1)}, bf16[256,1024]{1,0:T(8,128)(2,1)S(1)}, bf16[256,1024]{1,0:T(8,128)(2,1)S(1)}, f32[2,1024]{1,0:T(2,128)S(1)}) custom-call(bf16[256,1024]{1,0:T(8,128)(2,1)} %bitcast.7, bf16[256,1024]{1,0:T(8,128)(2,1)} %bitcast.8, bf16[256,1024]{1,0:T(8,128)(2,1)} %bitcast.9, bf16[256,1024]{1,0:T(8,128)(2,1)} %bitcast.10, ...), custom_call_target="tpu_custom_call" | custom-call | tf_op jit(solution)/shard_map/backward/pallas_call | solution.py:634
  57.3 1.2 %store.1 = (bf16[256,1024]{1,0:T(8,128)(2,1)}, bf16[256,1024]{1,0:T(8,128)(2,1)}, bf16[256,1024]{1,0:T(8,128)(2,1)}, f32[2,1024]{1,0:T(2,128)}) custom-call(bf16[256,1024]{1,0:T(8,128)(2,1)S(1)} %get-tuple-element.12.refs_0_, bf16[256,1024]{1,0:T(8,128)(2,1)S(1)} %get-tuple-element.13.refs_1_, bf16[256,1024]{1,0:T(8,128)(2,1)S(1)} %get-tuple-element.14.refs_2_, ...), custom_call_target="tpu_custom_call" | custom-call | tf_op jit(solution)/shard_map/store/pallas_call | solution.py:664

commit v5 on v4

--- a/solution.py
+++ b/solution.py
@@ -38,6 +38,15 @@
 
 def nn(left, right):
     return dot(left, right, ((1,), (0,)))
+
+
+def far_first(copies):
+    n = len(copies) + 1
+    if n == CHIPS:
+        return [copies[o - 1] for o in sorted(range(1, n), key=lambda o: -min(o % NY, NY - o % NY))]
+    if n == NY:
+        return [copies[o - 1] for o in sorted(range(1, n), key=lambda o: -min(o, n - o))]
+    return copies
 
 
 def head(h):
@@ -86,7 +95,7 @@
     sent, open_waits = [], {}
 
     def begin(name, make):
-        for copy in make():
+        for copy in far_first(make()):
             copy.start()
         open_waits[name] = lambda: [copy.wait_recv() for copy in make()]
         sent.append(lambda: [copy.wait_send() for copy in make()])

time: 58.6 us -> 56.6 us (0.966); the launches traced: 58.5 us -> 55.6 us
  Pallas kernels: 57.8 us -> 54.9 us
    pallas_call x1, Pallas kernels: 56.7 us -> 53.8 us  [per_device(): pl.pallas_call(body, out_shape=(out, out, out, jax.ShapeDtypeStruct((2, D...]
where the time goes in v5:
time: 56.6 us; the launch traced here: 55.6 us
  Pallas kernels  54.9 us (97%)
  between operations  0.64 us (1%)
    pallas_call x1, Pallas kernels, per_device(): pl.pallas_call(body, out_shape=(out, out, out, jax.ShapeDtypeStruct((2, D...  53.8 us
    pallas_call x1, Pallas kernels, per_device(): pl.pallas_call(store, out_shape=(out, out, out, jax.ShapeDtypeStruct((2,...  1.18 us

profile of v5, /device:TPU:1, one launch (start us, length us, event | category | flops | bytes accessed | tf_op | source)
XLA Modules:
  0.0 55.6 jit_solution(2224463094272993409)
XLA Ops:
  0.6 53.8 %backward.1 = (bf16[256,1024]{1,0:T(8,128)(2,1)S(1)}, bf16[256,1024]{1,0:T(8,128)(2,1)S(1)}, bf16[256,1024]{1,0:T(8,128)(2,1)S(1)}, f32[2,1024]{1,0:T(2,128)S(1)}) custom-call(bf16[256,1024]{1,0:T(8,128)(2,1)} %bitcast.7, bf16[256,1024]{1,0:T(8,128)(2,1)} %bitcast.8, bf16[256,1024]{1,0:T(8,128)(2,1)} %bitcast.9, bf16[256,1024]{1,0:T(8,128)(2,1)} %bitcast.10, ...), custom_call_target="tpu_custom_call" | custom-call | tf_op jit(solution)/shard_map/backward/pallas_call | solution.py:643
  54.4 1.2 %store.1 = (bf16[256,1024]{1,0:T(8,128)(2,1)}, bf16[256,1024]{1,0:T(8,128)(2,1)}, bf16[256,1024]{1,0:T(8,128)(2,1)}, f32[2,1024]{1,0:T(2,128)}) custom-call(bf16[256,1024]{1,0:T(8,128)(2,1)S(1)} %get-tuple-element.12.refs_0_, bf16[256,1024]{1,0:T(8,128)(2,1)S(1)} %get-tuple-element.13.refs_1_, bf16[256,1024]{1,0:T(8,128)(2,1)S(1)} %get-tuple-element.14.refs_2_, ...), custom_call_target="tpu_custom_call" | custom-call | tf_op jit(solution)/shard_map/store/pallas_call | solution.py:673
